TPU v7x, 32 devices: a whole 2x2x4 slice. The times are simulated.
32 devices in a mesh: batch: 8 (over z, y), head: 4 (over x, core).
Axes of the slice: x: 2, y: 2, z: 4, core: 2. Of those that a mesh axis runs over, the one named last changes fastest.
Arguments:
- tokens_in: bfloat16 [32768, 768], P(('batch', 'head')), may hold values from -5.6 to 5.6
- doc_ids: int32 [32768], P('batch'), may hold values from 0 to 3, as said below
- landmark_ids: int32 [32768], P('batch'), may hold values from 0 to 63, as said below
- pad_mask: int32 [32768], P('batch'), may hold values from 0 to 1, as said below
- w_query: bfloat16 [768, 768], P(None, 'head'), may hold values from -0.21875 to 0.21875
- w_key: bfloat16 [768, 768], P(None, 'head'), may hold values from -0.21875 to 0.21875
- w_value: bfloat16 [768, 768], P(None, 'head'), may hold values from -0.21875 to 0.21875
- w_output: bfloat16 [768, 768], P('head'), may hold values from -0.625 to 0.625
- conv_weight: bfloat16 [12, 33], P('head'), may hold values from -0.47851562 to 0.47851562
- first_gain: float32 [768], replicated, may hold values from 0.5 to 1.5
- first_bias: float32 [768], replicated, may hold values from -1.2 to 1.2
- w_inner: bfloat16 [768, 3072], replicated, may hold values from -0.21875 to 0.21875
- w_outer: bfloat16 [3072, 768], replicated, may hold values from -0.109375 to 0.109375
- second_gain: float32 [768], replicated, may hold values from 0.5 to 1.5
- second_bias: float32 [768], replicated, may hold values from -1.2 to 1.2
- out_grad: bfloat16 [32768, 768], P(('batch', 'head')), may hold values from -6 to 6
Outputs:
- layer_out: bfloat16 [32768, 768], P(('batch', 'head'))
- input_grad: bfloat16 [32768, 768], P(('batch', 'head'))
- grad_query: float32 [768, 768], P(None, 'head')
- grad_key: float32 [768, 768], P(None, 'head')
- grad_value: float32 [768, 768], P(None, 'head')
- grad_output: float32 [768, 768], P('head')
- grad_conv: float32 [12, 33], P('head')
- grad_first_gain: float32 [768], replicated
- grad_first_bias: float32 [768], replicated
- grad_inner: float32 [768, 3072], P(None, 'head')
- grad_outer: float32 [3072, 768], P('head')
- grad_second_gain: float32 [768], replicated
- grad_second_bias: float32 [768], replicated
Inputs may be any that keep to these rules, and one draw needn't show every extreme that they name: `doc_ids`: within a row of 4096 tokens document numbers never fall, and each document has 128 real tokens or more. `landmark_ids`: within a document landmark numbers never fall, and every landmark of every document has 2 or more real tokens. `pad_mask`: the padding of a row is its last tokens, at least one, and counts to its last document.
All inputs are finite; a program needn't handle non-finite values.
Results may differ from a plain program's by a relative error of at most 0.018.
Values may be sent and summed in bfloat16 or wider, within the bound.
No kernel may reach another device: no remote copies, remote signals or barrier semaphores. Data moves between devices by JAX's collectives and lax.ppermute only.
A program may use at most 256 MiB of HBM per device.

v0:
```python
import jax
import jax.numpy as jnp
from jax import lax
from jax.sharding import PartitionSpec as P

LAND = 64
KW = 33
HEAD_DIM = 64
NEWTON = 6
DOCS = 4
EXACT_PRECISION = lax.Precision.HIGHEST
NEG_FILL = -1e30
NORM_EPS = 1e-05


def newton_inverse(kernel):
    square_sum = jnp.sum(kernel * kernel, axis=(-2, -1), keepdims=True)
    estimate = jnp.swapaxes(kernel, -1, -2) / square_sum
    identity = jnp.eye(kernel.shape[-1], dtype=kernel.dtype)
    for step_count in range(NEWTON):
        product = jnp.matmul(kernel, estimate, precision=EXACT_PRECISION)
        factor_term = 7.0 * identity - product
        factor_term = 15.0 * identity - jnp.matmul(product, factor_term, precision=EXACT_PRECISION)
        factor_term = 13.0 * identity - jnp.matmul(product, factor_term, precision=EXACT_PRECISION)
        estimate = 0.25 * jnp.matmul(estimate, factor_term, precision=EXACT_PRECISION)
    return estimate


def norm_forward(hidden, scale_vec, shift_vec):
    center = hidden - jnp.mean(hidden, axis=-1, keepdims=True)
    inv_spread = lax.rsqrt(jnp.mean(center * center, axis=-1, keepdims=True) + NORM_EPS)
    normed = center * inv_spread
    return (normed * scale_vec + shift_vec, normed, inv_spread)


def norm_backward(upstream, normed, inv_spread, scale_vec):
    scaled = upstream * scale_vec
    result_grad = inv_spread * (
        scaled
        - jnp.mean(scaled, axis=-1, keepdims=True)
        - normed * jnp.mean(scaled * normed, axis=-1, keepdims=True)
    )
    return (result_grad, jnp.sum(upstream * normed, axis=0), jnp.sum(upstream, axis=0))


def exact_gelu(inputs):
    return jax.nn.gelu(inputs, approximate=False)


def softmax_back(prob_rows, upstream):
    return prob_rows * (upstream - jnp.sum(upstream * prob_rows, axis=-1, keepdims=True))


def shards(
    tokens_in,
    doc_ids,
    landmark_ids,
    pad_mask,
    w_query,
    w_key,
    w_value,
    w_output,
    conv_weight,
    first_gain,
    first_bias,
    w_inner,
    w_outer,
    second_gain,
    second_bias,
    out_grad,
):
    all_tokens = lax.all_gather(tokens_in, "head", axis=0, tiled=True)
    row_len = all_tokens.shape[0]
    local_heads = w_query.shape[1] // HEAD_DIM
    qk_scale = HEAD_DIM ** (-0.25)
    real_rows = pad_mask > 0
    real_float = real_rows.astype(jnp.float32)

    def project(weight, factor):
        mapped = jnp.dot(all_tokens, weight, preferred_element_type=jnp.float32) * factor
        return mapped.astype(jnp.bfloat16).reshape(row_len, local_heads, HEAD_DIM)

    queries = project(w_query, qk_scale)
    key_rows = project(w_key, qk_scale)
    values = project(w_value, 1.0)
    land_total = DOCS * LAND
    columns = jnp.arange(land_total, dtype=jnp.int32)
    segment = doc_ids * LAND + landmark_ids
    member = jnp.logical_and(segment[:, None] == columns[None, :], real_rows[:, None])
    member_float = member.astype(jnp.float32)
    member_low = member.astype(jnp.bfloat16)
    counts = jnp.sum(member_float, axis=0)
    same_doc = doc_ids[:, None] == (columns // LAND)[None, :]
    key_valid = jnp.logical_and(same_doc, real_rows[:, None])

    def landmark_mean(rows_in):
        summed_rows = jnp.einsum(
            "ts,thd->shd", member_low, rows_in, preferred_element_type=jnp.float32
        )
        return (summed_rows / counts[:, None, None]).astype(jnp.bfloat16)

    land_query = landmark_mean(queries)
    land_key = landmark_mean(key_rows)

    def first_scores():
        raw_scores = jnp.einsum(
            "thd,shd->hts", queries, land_key, preferred_element_type=jnp.float32
        )
        return jnp.where(same_doc[None], raw_scores, NEG_FILL)

    def third_scores():
        raw_scores = jnp.einsum(
            "shd,thd->hst", land_query, key_rows, preferred_element_type=jnp.float32
        )
        return jnp.where(key_valid.T[None], raw_scores, NEG_FILL)

    scores_now = first_scores()
    first_lse = jax.nn.logsumexp(scores_now, axis=-1, keepdims=True)
    first_low = jnp.exp(scores_now - first_lse).astype(jnp.bfloat16)
    scores_now = third_scores()
    third_lse = jax.nn.logsumexp(scores_now, axis=-1, keepdims=True)
    third_low = jnp.exp(scores_now - third_lse).astype(jnp.bfloat16)
    carried = jnp.einsum("hst,thd->hsd", third_low, values, preferred_element_type=jnp.float32)

    def small_kernel(land_q, land_k):
        doc_q = land_q.reshape(DOCS, LAND, local_heads, HEAD_DIM)
        doc_k = land_k.reshape(DOCS, LAND, local_heads, HEAD_DIM)
        small_scores = jnp.einsum("aihd,ajhd->haij", doc_q, doc_k, precision=EXACT_PRECISION)
        return newton_inverse(jax.nn.softmax(small_scores, axis=-1))

    inverse, inverse_pull = jax.vjp(
        small_kernel, land_query.astype(jnp.float32), land_key.astype(jnp.float32)
    )
    carried_docs = carried.reshape(local_heads, DOCS, LAND, HEAD_DIM)
    mixed_low = jnp.einsum("haij,hajd->haid", inverse, carried_docs, precision=EXACT_PRECISION)
    mixed_low = mixed_low.reshape(local_heads, land_total, HEAD_DIM).astype(jnp.bfloat16)
    attention = jnp.einsum("hts,hsd->thd", first_low, mixed_low, preferred_element_type=jnp.float32)
    half_width = KW // 2
    conv_float = conv_weight.astype(jnp.float32)
    padded_values = jnp.pad(values.astype(jnp.float32), ((half_width, half_width), (0, 0), (0, 0)))
    padded_docs = jnp.pad(doc_ids, (half_width, half_width), constant_values=-1)
    padded_real = jnp.pad(real_float, (half_width, half_width))
    valid_list = []
    conv_out = jnp.zeros(attention.shape, jnp.float32)
    for offset in range(KW):
        is_valid = jnp.where(
            padded_docs[offset : offset + row_len] == doc_ids,
            padded_real[offset : offset + row_len],
            0.0,
        )
        valid_list.append(is_valid)
        conv_out = conv_out + conv_float[:, offset][None, :, None] * (
            padded_values[offset : offset + row_len] * is_valid[:, None, None]
        )
    heads_out = ((attention + conv_out) * real_float[:, None, None]).astype(jnp.bfloat16)
    heads_out = heads_out.reshape(row_len, local_heads * HEAD_DIM)
    projected = lax.psum_scatter(
        jnp.dot(heads_out, w_output, preferred_element_type=jnp.float32).astype(jnp.bfloat16),
        "head",
        scatter_dimension=0,
        tiled=True,
    ).astype(jnp.float32)
    first_out, first_normed, first_inv = norm_forward(
        tokens_in.astype(jnp.float32) + projected, first_gain, first_bias
    )
    norm_low = first_out.astype(jnp.bfloat16)
    inner_pre = jnp.dot(norm_low, w_inner, preferred_element_type=jnp.float32)
    gelu_values, gelu_pull = jax.vjp(exact_gelu, inner_pre)
    inner_act = gelu_values.astype(jnp.bfloat16)
    outer_out = jnp.dot(inner_act, w_outer, preferred_element_type=jnp.float32)
    second_out, second_normed, second_inv = norm_forward(
        first_out + outer_out, second_gain, second_bias
    )
    layer_out = second_out.astype(jnp.bfloat16)
    second_grad, grad_second_gain, grad_second_bias = norm_backward(
        out_grad.astype(jnp.float32), second_normed, second_inv, second_gain
    )
    outer_low = second_grad.astype(jnp.bfloat16)
    act_grad = jnp.einsum("td,fd->tf", outer_low, w_outer, preferred_element_type=jnp.float32)
    pre_low = gelu_pull(act_grad)[0].astype(jnp.bfloat16)
    first_grad = second_grad + jnp.einsum(
        "tf,df->td", pre_low, w_inner, preferred_element_type=jnp.float32
    )
    first_in_grad, grad_first_gain, grad_first_bias = norm_backward(
        first_grad, first_normed, first_inv, first_gain
    )
    full_inner = jnp.einsum("td,tf->df", norm_low, pre_low, preferred_element_type=jnp.float32)
    full_outer = jnp.einsum("tf,td->fd", inner_act, outer_low, preferred_element_type=jnp.float32)
    grad_inner, grad_outer = (
        lax.psum_scatter(
            full_inner.astype(jnp.bfloat16), "head", scatter_dimension=1, tiled=True
        ).astype(jnp.float32),
        lax.psum_scatter(
            full_outer.astype(jnp.bfloat16), "head", scatter_dimension=0, tiled=True
        ).astype(jnp.float32),
    )
    proj_all = lax.all_gather(first_in_grad.astype(jnp.bfloat16), "head", axis=0, tiled=True)
    grad_output = jnp.einsum("tc,td->cd", heads_out, proj_all, preferred_element_type=jnp.float32)
    heads_grad = jnp.einsum("td,cd->tc", proj_all, w_output, preferred_element_type=jnp.float32)
    heads_grad = heads_grad.astype(jnp.bfloat16).reshape(row_len, local_heads, HEAD_DIM)
    heads_grad = jnp.where(real_rows[:, None, None], heads_grad, jnp.zeros_like(heads_grad))
    mixed_grad = jnp.einsum(
        "hts,thd->hsd", first_low, heads_grad, preferred_element_type=jnp.float32
    )
    first_prob = jnp.exp(first_scores() - first_lse)
    first_weight_grad = jnp.einsum(
        "thd,hsd->hts", heads_grad, mixed_low, preferred_element_type=jnp.float32
    )
    first_score_grad = softmax_back(first_prob, first_weight_grad).astype(jnp.bfloat16)
    grad_queries = jnp.einsum(
        "hts,shd->thd", first_score_grad, land_key, preferred_element_type=jnp.float32
    )
    land_key_grad = jnp.einsum(
        "hts,thd->shd", first_score_grad, queries, preferred_element_type=jnp.float32
    )
    mixed_docs = mixed_grad.reshape(local_heads, DOCS, LAND, HEAD_DIM)
    inverse_grad = jnp.einsum(
        "haid,hajd->haij", mixed_docs, carried_docs, precision=EXACT_PRECISION
    )
    carried_low = jnp.einsum("haij,haid->hajd", inverse, mixed_docs, precision=EXACT_PRECISION)
    carried_low = carried_low.reshape(local_heads, land_total, HEAD_DIM).astype(jnp.bfloat16)
    third_prob = jnp.exp(third_scores() - third_lse)
    third_weight_grad = jnp.einsum(
        "hsd,thd->hst", carried_low, values, preferred_element_type=jnp.float32
    )
    third_score_grad = softmax_back(third_prob, third_weight_grad).astype(jnp.bfloat16)
    land_query_grad = jnp.einsum(
        "hst,thd->shd", third_score_grad, key_rows, preferred_element_type=jnp.float32
    )
    grad_keys = jnp.einsum(
        "hst,shd->thd", third_score_grad, land_query, preferred_element_type=jnp.float32
    )
    grad_values = jnp.einsum(
        "hst,hsd->thd", third_low, carried_low, preferred_element_type=jnp.float32
    )
    small_query, small_key = inverse_pull(inverse_grad)
    land_query_grad = (land_query_grad + small_query) / counts[:, None, None]
    land_key_grad = (land_key_grad + small_key) / counts[:, None, None]
    grad_queries = grad_queries + jnp.einsum(
        "ts,shd->thd", member_float, land_query_grad, precision=EXACT_PRECISION
    )
    grad_keys = grad_keys + jnp.einsum(
        "ts,shd->thd", member_float, land_key_grad, precision=EXACT_PRECISION
    )
    heads_float = heads_grad.astype(jnp.float32)
    padded_heads = jnp.pad(heads_float, ((half_width, half_width), (0, 0), (0, 0)))
    conv_back = jnp.zeros(heads_float.shape, jnp.float32)
    conv_terms = []
    for offset in range(KW):
        weighted = heads_float * valid_list[offset][:, None, None]
        conv_terms.append(jnp.sum(weighted * padded_values[offset : offset + row_len], axis=(0, 2)))
        start = 2 * half_width - offset
        shifted_valid = jnp.pad(valid_list[offset], (half_width, half_width))[
            start : start + row_len
        ]
        shifted_weighted = padded_heads[start : start + row_len] * shifted_valid[:, None, None]
        conv_back = conv_back + shifted_weighted * conv_float[:, offset][None, :, None]
    grad_conv = jnp.stack(conv_terms, axis=1)
    grad_values = grad_values + conv_back
    query_low = grad_queries.astype(jnp.bfloat16).reshape(row_len, local_heads * HEAD_DIM)
    key_low = grad_keys.astype(jnp.bfloat16).reshape(row_len, local_heads * HEAD_DIM)
    value_low = grad_values.astype(jnp.bfloat16).reshape(row_len, local_heads * HEAD_DIM)
    grad_query = qk_scale * jnp.einsum(
        "tc,tk->ck", all_tokens, query_low, preferred_element_type=jnp.float32
    )
    grad_key = qk_scale * jnp.einsum(
        "tc,tk->ck", all_tokens, key_low, preferred_element_type=jnp.float32
    )
    grad_value = jnp.einsum("tc,tk->ck", all_tokens, value_low, preferred_element_type=jnp.float32)
    scaled_part = jnp.einsum("tc,dc->td", query_low, w_query, preferred_element_type=jnp.float32)
    scaled_part = scaled_part + jnp.einsum(
        "tc,dc->td", key_low, w_key, preferred_element_type=jnp.float32
    )
    attn_input = lax.psum_scatter(
        (
            qk_scale * scaled_part
            + jnp.einsum("tc,dc->td", value_low, w_value, preferred_element_type=jnp.float32)
        ).astype(jnp.bfloat16),
        "head",
        scatter_dimension=0,
        tiled=True,
    ).astype(jnp.float32)
    input_grad = (first_in_grad + attn_input).astype(jnp.bfloat16)
    summed = lax.psum(
        (grad_query, grad_key, grad_value, grad_output, grad_conv, grad_inner, grad_outer), "batch"
    )
    norm_totals = lax.psum(
        (grad_first_gain, grad_first_bias, grad_second_gain, grad_second_bias), ("batch", "head")
    )
    return (
        layer_out,
        input_grad,
        summed[0],
        summed[1],
        summed[2],
        summed[3],
        summed[4],
        norm_totals[0],
        norm_totals[1],
        summed[5],
        summed[6],
        norm_totals[2],
        norm_totals[3],
    )


def solution(mesh):
    placed = (
        P(("batch", "head"), None),
        P("batch"),
        P("batch"),
        P("batch"),
        P(None, "head"),
        P(None, "head"),
        P(None, "head"),
        P("head", None),
        P("head", None),
        P(),
        P(),
        P(),
        P(),
        P(),
        P(),
        P(("batch", "head"), None),
    )
    return jax.shard_map(
        shards,
        mesh=mesh,
        in_specs=placed,
        out_specs=(
            P(("batch", "head"), None),
            P(("batch", "head"), None),
            P(None, "head"),
            P(None, "head"),
            P(None, "head"),
            P("head", None),
            P("head", None),
            P(),
            P(),
            P(None, "head"),
            P("head", None),
            P(),
            P(),
        ),
        check_vma=False,
    )
```

profile of v0, /device:TPU:0, one launch (start us, length us, event | category | flops | bytes accessed | tf_op | source)
XLA Modules:
  0.0 913.9 jit_solution(11133062830195507953)
XLA Ops:
  24.1 34.7 %all-gather.3.cloned.1.call-done = bf16[4096,768]{1,0:T(8,128)(2,1)} async-done(((bf16[1024,768]{1,0:T(8,128)(2,1)}), bf16[4096,768]{1,0:T(8,128)(2,1)}) %all-gather.3.cloned.1.call-update) | async-done | bytes 6291472 | tf_op jit(solution)/shard_map/all_gather | solution.py:72
  85.9 12.5 %convolution_multiply_fusion.6 = f32[3,4,64,64]{3,2,1,0:T(8,128)S(1)} fusion(f32[3,4,64,64]{3,2,1,0:T(8,128)S(1)} %convolution_multiply_fusion.7, f32[3,4,64,64]{3,2,1,0:T(8,128)S(1)} %convolution_subtract_fusion.2), kind=kOutput, calls=%fused_computation.274 | convolution fusion | flops 37797888 | bytes 589824 | tf_op jit(solution)/shard_map/jvp()/dot_general | solution.py:25
  101.8 6.7 select_reduce_fusion.1
  108.5 8.1 exponential_reduce_fusion.1
  130.2 7.4 select_reduce_fusion
  137.7 7.2 exponential_reduce_fusion
  145.5 34.2 %fusion.14 = bf16[4096,3,64]{0,2,1:T(8,128)(2,1)} fusion(bf16[3,256,64]{2,1,0:T(8,128)(2,1)S(1)} %bitcast.347, f32[4096]{0:T(1024)} %get-tuple-element.146, f32[3]{0:T(128)} %get-tuple-element.67, f32[4096]{0:T(1024)} %get-tuple-element.145, f32[3]{0:T(128)} %get-tuple-element.68, f32[4096]{0:T(1024)} %get-tuple-element.144, f32[3]{0:T(128)} %get-tuple-element.69, ...), kind=kOutput, calls=%fused_computation.78 | convolution fusion | flops 492306432 | bytes 20611468 | tf_op jit(solution)/shard_map/hts,hsd->thd/dot_general | solution.py:137
  179.8 6.0 convolution_convert_fusion
  185.9 58.4 %reduce-scatter.5.cloned.1.call-done = bf16[1024,768]{1,0:T(8,128)(2,1)} async-done(((bf16[4096,768]{1,0:T(8,128)(2,1)}), bf16[1024,768]{1,0:T(8,128)(2,1)}) %reduce-scatter.5.cloned.1.call-update) | async-done | bytes 1572880 | tf_op jit(solution)/shard_map/reduce_scatter | solution.py:157
  247.2 37.5 %multiply_convert_fusion.2 = (bf16[1024,3072]{1,0:T(8,128)(2,1)S(1)}, f32[1024,3072]{1,0:T(8,128)}, f32[1024,3072]{1,0:T(8,128)}) fusion(bf16[768,3072]{1,0:T(8,128)(2,1)} %param.27, f32[768]{0:T(1024)S(1)} %copy-done.141, f32[768]{0:T(1024)S(1)} %copy-done.122, f32[1024]{0:T(1024)S(1)} %add_rsqrt_fusion.1, f32[1024]{0:T(1024)S(1)} %broadcast_multiply_fusion.5, ...), kind=kOutput, calls=%fused_computation.42 | convolution fusion | flops 5042601984 | bytes 39335936 | tf_op jit(solution)/shard_map/dot_general | solution.py:167
  296.2 17.6 %add_convert_fusion.1 = bf16[1024,3072]{1,0:T(8,128)(2,1)} fusion(f32[1024,3072]{1,0:T(8,128)} %get-tuple-element.111, f32[1024,3072]{1,0:T(8,128)} %get-tuple-element.155, bf16[3072,768]{1,0:T(8,128)(2,1)} %param.28, bf16[1024,768]{1,0:T(8,128)(2,1)} %param.31, f32[1024,768]{1,0:T(8,128)} %copy-done.26, f32[1024]{0:T(1024)S(1)} %broadcast_multiply_fusion.2, ...), kind=kOutput, calls=%fused_computation.41 | convolution fusion | flops 4882956288 | bytes 40913920 | tf_op jit(solution)/shard_map/td,fd->tf/dot_general | solution.py:179
  313.7 12.2 %multiply_reduce_fusion.2 = (f32[768]{0:T(1024)}, f32[1024]{0:T(1024)S(1)}, f32[1024]{0:T(1024)S(1)}, f32[768]{0:T(1024)}, f32[1024,768]{1,0:T(8,128)S(1)}) fusion(f32[1024]{0:T(1024)S(1)} %add_rsqrt_fusion.1, f32[1024]{0:T(1024)S(1)} %broadcast_multiply_fusion.5, bf16[1024,768]{1,0:T(8,128)(2,1)S(1)} %copy-done.10, bf16[1024,768]{1,0:T(8,128)(2,1)S(1)} %copy-done.6, ...), kind=kOutput, calls=%fused_computation.186 | convolution fusion | flops 4848349184 | bytes 22065152 | tf_op jit(solution)/shard_map/tf,df->td/dot_general | solution.py:181
  329.9 12.1 %convolution_convert_fusion.1 = bf16[3072,768]{1,0:T(8,128)(2,1)} fusion(bf16[1024,3072]{1,0:T(8,128)(2,1)} %copy-done.142, bf16[1024,768]{1,0:T(8,128)(2,1)} %param.31, f32[1024,768]{1,0:T(8,128)} %copy-done.26, f32[1024]{0:T(1024)S(1)} %broadcast_multiply_fusion.2, f32[1024]{0:T(1024)S(1)} %broadcast_multiply_fusion.3, f32[768]{0:T(1024)S(1)} %copy-done.136, ...), kind=kOutput, calls=%fused_computation.76 | convolution fusion | flops 4841275392 | bytes 15748096 | tf_op jit(solution)/shard_map/tf,td->fd/dot_general | solution.py:188
  366.0 10.2 %convolution_convert_fusion.2 = bf16[768,3072]{1,0:T(8,128)(2,1)} fusion(bf16[1024,3072]{1,0:T(8,128)(2,1)} %add_convert_fusion.1, f32[768]{0:T(1024)S(1)} %copy-done.141, f32[768]{0:T(1024)S(1)} %copy-done.122, bf16[1024,768]{1,0:T(8,128)(2,1)S(1)} %copy-done.10, bf16[1024,768]{1,0:T(8,128)(2,1)S(1)} %copy-done.6, f32[1024]{0:T(1024)S(1)} %add_rsqrt_fusion.1, ...), kind=kOutput, calls=%fused_computation.77 | convolution fusion | flops 4840488960 | bytes 14170112 | tf_op jit(solution)/shard_map/td,tf->df/dot_general | solution.py:187
  377.0 6.1 multiply_reduce_fusion.3
  383.1 9.0 fusion.175
  426.8 8.7 multiply_reduce_fusion.1
  445.6 10.8 %multiply_reduce_fusion = (f32[3,256]{1,0:T(4,128)S(1)}, f32[3,256,4096]{2,1,0:T(8,128)}) fusion(f32[3,256,4096]{2,1,0:T(8,128)} %get-tuple-element.152, f32[3,256]{1,0:T(4,128)S(1)} %copy-done.111, pred[256,4096]{1,0:T(8,128)(4,1)S(1)} %copy-done.5, bf16[3,256,64]{2,1,0:T(8,128)(2,1)S(1)} %bitcast.343, bf16[4096,3,64]{0,2,1:T(8,128)(2,1)} %bitcast.328), kind=kOutput, calls=%fused_computation.38 | convolution fusion | flops 415235328 | bytes 27891712 | tf_op jit(solution)/shard_map/hsd,thd->hst/dot_general | solution.py:223
  458.2 10.2 %multiply_convert_fusion.1 = bf16[3,4096,256]{1,2,0:T(8,128)(2,1)S(1)} fusion(f32[3,4096,256]{1,2,0:T(8,128)} %get-tuple-element.166, f32[3,4096,256]{1,2,0:T(8,128)} %get-tuple-element.154, f32[3,4096]{1,0:T(4,128)S(1)} %copy-done.109, f32[3,4096]{1,0:T(4,128)S(1)} %copy-done.95, pred[4096,256]{0,1:T(8,128)(4,1)} %broadcast_compare_fusion), kind=kLoop, calls=%fused_computation.39 | loop fusion | flops 15728640 | bytes 32604160 | tf_op jit(solution)/shard_map/convert_element_type | solution.py:209
  470.5 7.5 multiply_convert_fusion
  480.1 5.9 fusion.24
  488.1 5.9 fusion.26
  496.7 6.5 fusion.295
  503.1 6.3 fusion.294
  511.4 58.6 %fusion.17 = bf16[4096,3,64]{0,2,1:T(8,128)(2,1)S(1)} fusion(bf16[3,256,64]{2,1,0:T(8,128)(2,1)S(1)} %bitcast.344, f32[4096,3,64]{0,2,1:T(8,128)} %fusion.270, f32[4096]{0:T(1024)} %get-tuple-element.171, f32[4096]{0:T(1024)} %get-tuple-element.172, f32[4096]{0:T(1024)} %get-tuple-element.173, f32[4096]{0:T(1024)} %get-tuple-element.174, ...), kind=kOutput, calls=%fused_computation.81 | convolution fusion | flops 492306432 | bytes 20569484 | tf_op jit(solution)/shard_map/hst,hsd->thd/dot_general | solution.py:233
  571.2 12.4 %add_convert_fusion = bf16[4096,768]{1,0:T(8,128)(2,1)} fusion(f32[4096,768]{1,0:T(8,128)} %fusion.294, f32[4096,768]{1,0:T(8,128)} %fusion.295, bf16[4096,192]{0,1:T(8,128)(2,1)S(1)} %bitcast.337, bf16[768,192]{0,1:T(8,128)(2,1)S(1)} %copy-done.104), kind=kOutput, calls=%fused_computation.36 | convolution fusion | flops 1220542464 | bytes 33325056 | tf_op jit(solution)/shard_map/tc,dc->td/dot_general | solution.py:277
  584.3 40.5 %all-reduce.36 = (f32[768]{0:T(1024)}, f32[768]{0:T(1024)}, f32[768]{0:T(1024)}, f32[768]{0:T(1024)}) all-reduce(f32[768]{0:T(1024)S(1)} %copy-done.137, f32[768]{0:T(1024)S(1)} %copy-done.138, f32[768]{0:T(1024)S(1)} %copy-done.124, f32[768]{0:T(1024)S(1)} %copy-done.125), channel_id=1, replica_groups=mesh['batch'=8,'head'=4] {'batch','head'}, use_global_device_ids=true, to_apply=%region_62.63 | all-reduce | flops 3072 | bytes 24576 | tf_op jit(solution)/shard_map/psum | solution.py:287
  624.9 8.3 fusion.117
  633.8 8.3 fusion.115
  658.2 8.3 fusion.113
  668.6 9.2 %fusion.111 = (f32[3]{0:T(128)}, f32[3]{0:T(128)}, f32[3]{0:T(128)}, f32[3]{0:T(128)}, f32[3]{0:T(128)}, /*index=5*/f32[3]{0:T(128)}, f32[3]{0:T(128)}, f32[3]{0:T(128)}) fusion(f32[4096]{0:T(1024)} %get-tuple-element.143, f32[4096,3,64]{0,2,1:T(8,128)S(1)} %copy-done.2, bf16[4096,3,64]{0,2,1:T(8,128)(2,1)} %bitcast.320, pred[4096]{0:T(1024)(128)(4,1)S(1)} %copy-done.91, ...), kind=kLoop, calls=%fused_computation.179 | loop fusion | flops 20447208 | bytes 4853856 | tf_op jit(solution)/shard_map/reduce_sum | solution.py:251
  685.5 209.9 %all-reduce.43 = (f32[3,33]{1,0:T(4,128)}, f32[768,768]{1,0:T(8,128)}, f32[768,768]{1,0:T(8,128)}) all-reduce(f32[3,33]{1,0:T(4,128)S(1)} %stack.135, bf16[768,768]{1,0:T(8,128)(2,1)} %reduce-scatter.9.cloned.1.call-done, bf16[768,768]{1,0:T(8,128)(2,1)} %reduce-scatter.11.cloned.1.call-done), channel_id=1, replica_groups=mesh['batch'=8,'head'=4] {'batch'}, use_global_device_ids=true, to_apply=%region_60.61 | all-reduce | flops 1179747 | bytes 7078680 | tf_op jit(solution)/shard_map/psum | solution.py:284
  (535 shorter events, 199.4 us)
Async XLA Ops:
  7.2 172.6 %copy-start = (bf16[192,768]{1,0:T(8,128)(2,1)S(1)}, bf16[192,768]{1,0:T(8,128)(2,1)}, u32[]{:S(2)}) copy-start(bf16[192,768]{1,0:T(8,128)(2,1)} %param.23) | copy-start | bytes 884740
  7.2 51.5 %copy-start.107 = (bf16[768,192]{0,1:T(8,128)(2,1)S(1)}, bf16[768,192]{0,1:T(8,128)(2,1)}, u32[]{:S(2)}) copy-start(bf16[768,192]{0,1:T(8,128)(2,1)} %param.20) | copy-start | bytes 884740
  7.2 51.5 %all-gather.3.cloned.1.call-start = ((), (), s32[]{:S(2)}) async-start(), calls=%async_computation.4 | async-start | bytes 7864320 | tf_op jit(solution)/shard_map/all_gather | solution.py:72
  8.0 236.4 %reduce-scatter.5.cloned.1.call-start = ((), (), s32[]{:S(2)}) async-start(), calls=%async_computation.5 | async-start | bytes 7864320 | tf_op jit(solution)/shard_map/reduce_scatter | solution.py:157
  10.6 88.6 %copy-start.44 = (f32[64,64]{1,0:T(8,128)}, f32[64,64]{1,0:T(8,128)S(1)}, u32[]{:S(2)}) copy-start(f32[64,64]{1,0:T(8,128)S(1)} %get-tuple-element.169) | copy-start | bytes 49156
  11.4 56.1 %copy-start.90 = (pred[4096]{0:T(1024)(128)(4,1)}, pred[4096]{0:T(1024)(128)(4,1)S(1)}, u32[]{:S(2)}) copy-start(pred[4096]{0:T(1024)(128)(4,1)S(1)} %get-tuple-element.113) | copy-start | bytes 12292
  11.4 134.1 %copy-start.99 = (f32[4096]{0:T(1024)}, f32[4096]{0:T(1024)S(1)}, u32[]{:S(2)}) copy-start(f32[4096]{0:T(1024)S(1)} %get-tuple-element.112) | copy-start | bytes 49156
  12.1 55.3 %copy-start.96 = (s32[4096]{0:T(1024)}, s32[4096]{0:T(1024)S(1)}, u32[]{:S(2)}) copy-start(s32[4096]{0:T(1024)S(1)} %multiply_add_fusion.1) | copy-start | bytes 49156
  13.6 55.3 %copy-start.120 = (f32[256]{0:T(256)}, f32[256]{0:T(256)S(1)}, u32[]{:S(2)}) copy-start(f32[256]{0:T(256)S(1)} %convert_reduce_fusion.1) | copy-start | bytes 3076
  24.0 77.7 %copy-start.4 = (pred[256,4096]{1,0:T(8,128)(4,1)}, pred[256,4096]{1,0:T(8,128)(4,1)S(1)}, u32[]{:S(2)}) copy-start(pred[256,4096]{1,0:T(8,128)(4,1)S(1)} %compare_and_fusion) | copy-start | bytes 3145732
  68.9 61.3 %copy-start.75 = (bf16[256,3,64]{0,2,1:T(8,128)(2,1)}, bf16[256,3,64]{0,2,1:T(8,128)(2,1)S(1)}, u32[]{:S(2)}) copy-start(bf16[256,3,64]{0,2,1:T(8,128)(2,1)S(1)} %get-tuple-element.147) | copy-start | bytes 294916
  185.8 58.5 %copy-start.6 = (bf16[1024,768]{1,0:T(8,128)(2,1)S(1)}, bf16[1024,768]{1,0:T(8,128)(2,1)}, u32[]{:S(2)}) copy-start(bf16[1024,768]{1,0:T(8,128)(2,1)} %param.16) | copy-start | bytes 4718596
  185.8 61.3 %copy-start.122 = (f32[768]{0:T(1024)S(1)}, f32[768]{0:T(1024)}, u32[]{:S(2)}) copy-start(f32[768]{0:T(1024)} %param.25) | copy-start | bytes 9220
  185.8 61.3 %copy-start.141 = (f32[768]{0:T(1024)S(1)}, f32[768]{0:T(1024)}, u32[]{:S(2)}) copy-start(f32[768]{0:T(1024)} %param.26) | copy-start | bytes 9220
  185.8 190.7 %all-gather.5.cloned.1.call-start = ((), (), s32[]{:S(2)}) async-start(), calls=%async_computation.6 | async-start | bytes 7864320 | tf_op jit(solution)/shard_map/all_gather | solution.py:197
  244.3 40.4 %slice-start.13 = ((s8[4718592]{0:T(1024)(128)(4,1)}), s8[4194304]{0:T(1024)(128)(4,1)S(1)}, s32[]{:S(2)}) async-start(s8[4718592]{0:T(1024)(128)(4,1)} %bitcast.394), calls=%async_computation.24 | async-start | bytes 8388608
  246.4 119.6 %copy-start.112 = (f32[1024]{0:T(1024)}, f32[1024]{0:T(1024)S(1)}, u32[]{:S(2)}) copy-start(f32[1024]{0:T(1024)S(1)} %broadcast_multiply_fusion.5) | copy-start | bytes 12292
  247.2 118.8 %copy-start.114 = (f32[1024]{0:T(1024)}, f32[1024]{0:T(1024)S(1)}, u32[]{:S(2)}) copy-start(f32[1024]{0:T(1024)S(1)} %add_rsqrt_fusion.1) | copy-start | bytes 12292
  247.2 37.5 %slice-start.14 = ((s8[4718592]{0:T(1024)(128)(4,1)}), s8[524288]{0:T(1024)(128)(4,1)S(1)}, s32[]{:S(2)}) async-start(s8[4718592]{0:T(1024)(128)(4,1)} %bitcast.394), calls=%async_computation.25 | async-start | bytes 1048576
  329.8 355.7 %reduce-scatter.11.cloned.1.call-start = ((), (), s32[]{:S(2)}) async-start(), calls=%async_computation.9 | async-start | bytes 5898240 | tf_op jit(solution)/shard_map/reduce_scatter | solution.py:193
  342.0 343.5 %reduce-scatter.9.cloned.1.call-start = ((), (), s32[]{:S(2)}) async-start(), calls=%async_computation.8 | async-start | bytes 5898240 | tf_op jit(solution)/shard_map/reduce_scatter | solution.py:190
  376.3 519.1 %reduce-scatter.7.cloned.1.call-start = ((), (), s32[]{:S(2)}) async-start(), calls=%async_computation.7 | async-start | bytes 7864320 | tf_op jit(solution)/shard_map/reduce_scatter | solution.py:274
  383.1 128.3 %copy-start.3 = (bf16[4096,192]{0,1:T(8,128)(2,1)}, bf16[4096,192]{0,1:T(8,128)(2,1)S(1)}, u32[]{:S(2)}) copy-start(bf16[4096,192]{0,1:T(8,128)(2,1)S(1)} %get-tuple-element.168) | copy-start | bytes 4718596
  511.4 59.8 %copy-start.104 = (bf16[768,192]{0,1:T(8,128)(2,1)S(1)}, bf16[768,192]{0,1:T(8,128)(2,1)}, u32[]{:S(2)}) copy-start(bf16[768,192]{0,1:T(8,128)(2,1)} %param.22) | copy-start | bytes 884740
  583.6 41.2 %copy-start.2 = (f32[4096,3,64]{0,2,1:T(8,128)S(1)}, f32[4096,3,64]{0,2,1:T(8,128)}, u32[]{:S(2)}) copy-start(f32[4096,3,64]{0,2,1:T(8,128)} %convert_element_type.180) | copy-start | bytes 9437188
  583.7 316.3 %all-reduce.42.cloned.1.call-start = ((), (), s32[]{:S(2)}) async-start(), calls=%async_computation.10 | async-start | bytes 4718592 | tf_op jit(solution)/shard_map/psum | solution.py:284
  668.6 226.8 %copy-start.113 = (f32[1024]{0:T(1024)S(1)}, f32[1024]{0:T(1024)}, u32[]{:S(2)}) copy-start(f32[1024]{0:T(1024)} %copy-done.112) | copy-start | bytes 12292
  668.6 226.8 %copy-start.115 = (f32[1024]{0:T(1024)S(1)}, f32[1024]{0:T(1024)}, u32[]{:S(2)}) copy-start(f32[1024]{0:T(1024)} %copy-done.114) | copy-start | bytes 12292
  668.6 226.8 %copy-start.117 = (f32[1024]{0:T(1024)S(1)}, f32[1024]{0:T(1024)}, u32[]{:S(2)}) copy-start(f32[1024]{0:T(1024)} %copy-done.116) | copy-start | bytes 12292
  668.6 226.8 %copy-start.119 = (f32[1024]{0:T(1024)S(1)}, f32[1024]{0:T(1024)}, u32[]{:S(2)}) copy-start(f32[1024]{0:T(1024)} %copy-done.118) | copy-start | bytes 12292
  668.6 226.9 %copy-start.123 = (f32[768]{0:T(1024)S(1)}, f32[768]{0:T(1024)}, u32[]{:S(2)}) copy-start(f32[768]{0:T(1024)} %param.25) | copy-start | bytes 9220
  677.8 217.6 %copy-start.7 = (bf16[1024,768]{1,0:T(8,128)(2,1)S(1)}, bf16[1024,768]{1,0:T(8,128)(2,1)}, u32[]{:S(2)}) copy-start(bf16[1024,768]{1,0:T(8,128)(2,1)} %param.16) | copy-start | bytes 4718596
  (133 other events, 876.7 us)
Sparse Core Ops, SparseCore 0:
  9.6 49.0 all-gather.2
  185.9 58.3 reduce-scatter.4
  330.0 46.4 all-gather.4
  379.0 47.8 reduce-scatter.10
  429.3 47.8 reduce-scatter.8
  583.8 59.5 reduce-scatter.6
  658.3 148.6 all-reduce.41
where the time goes:
time: 925 us; the launch traced here: 914 us
  matrix products  393 us (42%)
  blocking collectives  250 us (27%)
  other arithmetic  101 us (11%)
  waiting for transfers between devices  94.1 us (10%)
  local copies, waits for them, and re-layouts  57.7 us (6%)
  between operations  17.2 us (2%)
    psum x1, blocking collectives, shards(): lax.psum((grad_query, grad_key, grad_value, grad_output, grad_conv, grad_...  210 us
    dot_general x1, matrix products, shards(): jnp.einsum('hst,hsd->thd', third_low, carried_low, preferred_element_type...  58.6 us
    reduce_scatter x1, waiting for transfers between devices, shards(): lax.psum_scatter(jnp.dot(heads_out, w_output, preferred_element_type=jnp....  58.4 us
    psum x1, blocking collectives, shards(): lax.psum((grad_first_gain, grad_first_bias, grad_second_gain, grad_second...  40.5 us
    dot_general x1, matrix products, shards(): inner_pre = jnp.dot(norm_low, w_inner, preferred_element_type=jnp.float32)  37.5 us
    all_gather x1, waiting for transfers between devices, shards(): all_tokens = lax.all_gather(tokens_in, 'head', axis=0, tiled=True)  34.7 us
    reduce_sum x5, other arithmetic, shards(): jnp.sum(weighted * padded_values[offset:offset + row_len], axis=(0, 2))  34.2 us
    dot_general x1, matrix products, shards(): jnp.einsum('hts,hsd->thd', first_low, mixed_low, preferred_element_type=j...  34.2 us
  transfers between devices with their start and end apart: 7, of which 3 were waited for; matrix products, arithmetic and copies ran while one was open for 36% of the time, Pallas kernels for 0%

commit v1 on v0

--- a/solution.py
+++ b/solution.py
@@ -285,7 +285,8 @@
         (grad_query, grad_key, grad_value, grad_output, grad_conv, grad_inner, grad_outer), "batch"
     )
     norm_totals = lax.psum(
-        (grad_first_gain, grad_first_bias, grad_second_gain, grad_second_bias), ("batch", "head")
+        lax.psum((grad_first_gain, grad_first_bias, grad_second_gain, grad_second_bias), "head"),
+        "batch",
     )
     return (
         layer_out,

time: 925 us -> 895 us (0.968)
  blocking collectives: 250 us -> 220 us
    psum x1, blocking collectives: 40.5 us -> 11.1 us  [shards(): lax.psum((grad_first_gain, grad_first_bias, grad_second_gain, grad_second...]
  transfers between devices with their start and end apart: 7 -> 7, of which waited for: 3 -> 3; matrix products, arithmetic and copies ran while one was open for 36% -> 37% of each run, Pallas kernels for 0% -> 0%
where the time goes in v1:
time: 895 us; the launch traced here: 884 us
  matrix products  393 us (44%)
  blocking collectives  220 us (25%)
  other arithmetic  101 us (11%)
  waiting for transfers between devices  94.1 us (11%)
  local copies, waits for them, and re-layouts  57.7 us (6%)
  between operations  17.2 us (2%)
    psum x1, blocking collectives, shards(): lax.psum((grad_query, grad_key, grad_value, grad_output, grad_conv, grad_...  209 us
    dot_general x1, matrix products, shards(): jnp.einsum('hst,hsd->thd', third_low, carried_low, preferred_element_type...  58.6 us
    reduce_scatter x1, waiting for transfers between devices, shards(): lax.psum_scatter(jnp.dot(heads_out, w_output, preferred_element_type=jnp....  58.4 us
    dot_general x1, matrix products, shards(): inner_pre = jnp.dot(norm_low, w_inner, preferred_element_type=jnp.float32)  37.5 us
    all_gather x1, waiting for transfers between devices, shards(): all_tokens = lax.all_gather(tokens_in, 'head', axis=0, tiled=True)  34.7 us
    reduce_sum x5, other arithmetic, shards(): jnp.sum(weighted * padded_values[offset:offset + row_len], axis=(0, 2))  34.4 us
    dot_general x1, matrix products, shards(): jnp.einsum('hts,hsd->thd', first_low, mixed_low, preferred_element_type=j...  34.2 us
    dot_general x18, matrix products, newton_inverse(): jnp.matmul(estimate, factor_term, precision=EXACT_PRECISION)  26.2 us
  transfers between devices with their start and end apart: 7, of which 3 were waited for; matrix products, arithmetic and copies ran while one was open for 37% of the time, Pallas kernels for 0%

profile of v1, /device:TPU:0, one launch (start us, length us, event | category | flops | bytes accessed | tf_op | source)
XLA Modules:
  0.0 884.0 jit_solution(6286977714259474386)
XLA Ops:
  24.1 34.7 %all-gather.3.cloned.1.call-done = bf16[4096,768]{1,0:T(8,128)(2,1)} async-done(((bf16[1024,768]{1,0:T(8,128)(2,1)}), bf16[4096,768]{1,0:T(8,128)(2,1)}) %all-gather.3.cloned.1.call-update) | async-done | bytes 6291472 | tf_op jit(solution)/shard_map/all_gather | solution.py:72
  85.9 12.5 %convolution_multiply_fusion.6 = f32[3,4,64,64]{3,2,1,0:T(8,128)S(1)} fusion(f32[3,4,64,64]{3,2,1,0:T(8,128)S(1)} %convolution_multiply_fusion.7, f32[3,4,64,64]{3,2,1,0:T(8,128)S(1)} %convolution_subtract_fusion.2), kind=kOutput, calls=%fused_computation.274 | convolution fusion | flops 37797888 | bytes 589824 | tf_op jit(solution)/shard_map/jvp()/dot_general | solution.py:25
  101.8 6.7 select_reduce_fusion.1
  108.5 8.1 exponential_reduce_fusion.1
  130.2 7.4 select_reduce_fusion
  137.7 7.2 exponential_reduce_fusion
  145.5 34.2 %fusion.14 = bf16[4096,3,64]{0,2,1:T(8,128)(2,1)} fusion(bf16[3,256,64]{2,1,0:T(8,128)(2,1)S(1)} %bitcast.347, f32[4096]{0:T(1024)} %get-tuple-element.150, f32[3]{0:T(128)} %get-tuple-element.67, f32[4096]{0:T(1024)} %get-tuple-element.149, f32[3]{0:T(128)} %get-tuple-element.68, f32[4096]{0:T(1024)} %get-tuple-element.148, f32[3]{0:T(128)} %get-tuple-element.69, ...), kind=kOutput, calls=%fused_computation.78 | convolution fusion | flops 492306432 | bytes 20611468 | tf_op jit(solution)/shard_map/hts,hsd->thd/dot_general | solution.py:137
  179.8 6.0 convolution_convert_fusion
  185.9 58.4 %reduce-scatter.5.cloned.1.call-done = bf16[1024,768]{1,0:T(8,128)(2,1)} async-done(((bf16[4096,768]{1,0:T(8,128)(2,1)}), bf16[1024,768]{1,0:T(8,128)(2,1)}) %reduce-scatter.5.cloned.1.call-update) | async-done | bytes 1572880 | tf_op jit(solution)/shard_map/reduce_scatter | solution.py:157
  247.2 37.5 %multiply_convert_fusion.2 = (bf16[1024,3072]{1,0:T(8,128)(2,1)S(1)}, f32[1024,3072]{1,0:T(8,128)}, f32[1024,3072]{1,0:T(8,128)}) fusion(bf16[768,3072]{1,0:T(8,128)(2,1)} %param.27, f32[768]{0:T(1024)S(1)} %copy-done.141, f32[768]{0:T(1024)S(1)} %copy-done.122, f32[1024]{0:T(1024)S(1)} %add_rsqrt_fusion.1, f32[1024]{0:T(1024)S(1)} %broadcast_multiply_fusion.5, ...), kind=kOutput, calls=%fused_computation.42 | convolution fusion | flops 5042601984 | bytes 39335936 | tf_op jit(solution)/shard_map/dot_general | solution.py:167
  296.2 17.6 %add_convert_fusion.1 = bf16[1024,3072]{1,0:T(8,128)(2,1)} fusion(f32[1024,3072]{1,0:T(8,128)} %get-tuple-element.115, f32[1024,3072]{1,0:T(8,128)} %get-tuple-element.159, bf16[3072,768]{1,0:T(8,128)(2,1)} %param.28, bf16[1024,768]{1,0:T(8,128)(2,1)} %param.31, f32[1024,768]{1,0:T(8,128)} %copy-done.26, f32[1024]{0:T(1024)S(1)} %broadcast_multiply_fusion.2, ...), kind=kOutput, calls=%fused_computation.41 | convolution fusion | flops 4882956288 | bytes 40913920 | tf_op jit(solution)/shard_map/td,fd->tf/dot_general | solution.py:179
  313.7 12.2 %multiply_reduce_fusion.2 = (f32[768]{0:T(1024)}, f32[1024]{0:T(1024)S(1)}, f32[1024]{0:T(1024)S(1)}, f32[768]{0:T(1024)}, f32[1024,768]{1,0:T(8,128)S(1)}) fusion(f32[1024]{0:T(1024)S(1)} %add_rsqrt_fusion.1, f32[1024]{0:T(1024)S(1)} %broadcast_multiply_fusion.5, bf16[1024,768]{1,0:T(8,128)(2,1)S(1)} %copy-done.10, bf16[1024,768]{1,0:T(8,128)(2,1)S(1)} %copy-done.6, ...), kind=kOutput, calls=%fused_computation.186 | convolution fusion | flops 4848349184 | bytes 22065152 | tf_op jit(solution)/shard_map/tf,df->td/dot_general | solution.py:181
  329.9 12.1 %convolution_convert_fusion.1 = bf16[3072,768]{1,0:T(8,128)(2,1)} fusion(bf16[1024,3072]{1,0:T(8,128)(2,1)} %copy-done.142, bf16[1024,768]{1,0:T(8,128)(2,1)} %param.31, f32[1024,768]{1,0:T(8,128)} %copy-done.26, f32[1024]{0:T(1024)S(1)} %broadcast_multiply_fusion.2, f32[1024]{0:T(1024)S(1)} %broadcast_multiply_fusion.3, f32[768]{0:T(1024)S(1)} %copy-done.136, ...), kind=kOutput, calls=%fused_computation.76 | convolution fusion | flops 4841275392 | bytes 15748096 | tf_op jit(solution)/shard_map/tf,td->fd/dot_general | solution.py:188
  366.0 10.2 %convolution_convert_fusion.2 = bf16[768,3072]{1,0:T(8,128)(2,1)} fusion(bf16[1024,3072]{1,0:T(8,128)(2,1)} %add_convert_fusion.1, f32[768]{0:T(1024)S(1)} %copy-done.141, f32[768]{0:T(1024)S(1)} %copy-done.122, bf16[1024,768]{1,0:T(8,128)(2,1)S(1)} %copy-done.10, bf16[1024,768]{1,0:T(8,128)(2,1)S(1)} %copy-done.6, f32[1024]{0:T(1024)S(1)} %add_rsqrt_fusion.1, ...), kind=kOutput, calls=%fused_computation.77 | convolution fusion | flops 4840488960 | bytes 14170112 | tf_op jit(solution)/shard_map/td,tf->df/dot_general | solution.py:187
  377.0 6.1 multiply_reduce_fusion.3
  383.1 9.0 %fusion.175 = f32[3,256,64]{2,1,0:T(8,128)S(1)} fusion(f32[3,4096,256]{1,2,0:T(8,128)} %get-tuple-element.158, f32[3,4096]{1,0:T(4,128)S(1)} %copy-done.93, pred[4096,256]{0,1:T(8,128)(4,1)S(1)} %copy-done.9, bf16[4096,3,64]{0,2,1:T(8,128)(2,1)S(1)} %bitcast.313, pred[4096]{0:T(1024)(128)(4,1)S(1)} %copy-done.91), kind=kOutput, calls=%fused_computation.320 | convolution fusion | flops 412876800 | bytes 15454208 | tf_op jit(solution)/shard_map/reshape | solution.py:216
  426.8 8.7 multiply_reduce_fusion.1
  445.6 10.8 %multiply_reduce_fusion = (f32[3,256]{1,0:T(4,128)S(1)}, f32[3,256,4096]{2,1,0:T(8,128)}) fusion(f32[3,256,4096]{2,1,0:T(8,128)} %get-tuple-element.156, f32[3,256]{1,0:T(4,128)S(1)} %copy-done.111, pred[256,4096]{1,0:T(8,128)(4,1)S(1)} %copy-done.5, bf16[3,256,64]{2,1,0:T(8,128)(2,1)S(1)} %bitcast.343, bf16[4096,3,64]{0,2,1:T(8,128)(2,1)} %bitcast.328), kind=kOutput, calls=%fused_computation.38 | convolution fusion | flops 415235328 | bytes 27891712 | tf_op jit(solution)/shard_map/hsd,thd->hst/dot_general | solution.py:223
  458.2 10.2 %multiply_convert_fusion.1 = bf16[3,4096,256]{1,2,0:T(8,128)(2,1)S(1)} fusion(f32[3,4096,256]{1,2,0:T(8,128)} %get-tuple-element.170, f32[3,4096,256]{1,2,0:T(8,128)} %get-tuple-element.158, f32[3,4096]{1,0:T(4,128)S(1)} %copy-done.109, f32[3,4096]{1,0:T(4,128)S(1)} %copy-done.95, pred[4096,256]{0,1:T(8,128)(4,1)} %broadcast_compare_fusion), kind=kLoop, calls=%fused_computation.39 | loop fusion | flops 15728640 | bytes 32604160 | tf_op jit(solution)/shard_map/convert_element_type | solution.py:209
  470.5 7.5 multiply_convert_fusion
  480.1 5.9 fusion.24
  488.1 5.9 fusion.26
  496.7 6.5 fusion.295
  503.1 6.3 fusion.294
  511.4 58.6 %fusion.17 = bf16[4096,3,64]{0,2,1:T(8,128)(2,1)S(1)} fusion(bf16[3,256,64]{2,1,0:T(8,128)(2,1)S(1)} %bitcast.344, f32[4096,3,64]{0,2,1:T(8,128)} %fusion.270, f32[4096]{0:T(1024)} %get-tuple-element.175, f32[4096]{0:T(1024)} %get-tuple-element.176, f32[4096]{0:T(1024)} %get-tuple-element.177, f32[4096]{0:T(1024)} %get-tuple-element.178, ...), kind=kOutput, calls=%fused_computation.81 | convolution fusion | flops 492306432 | bytes 20569484 | tf_op jit(solution)/shard_map/hst,hsd->thd/dot_general | solution.py:233
  571.2 12.4 %add_convert_fusion = bf16[4096,768]{1,0:T(8,128)(2,1)} fusion(f32[4096,768]{1,0:T(8,128)} %fusion.294, f32[4096,768]{1,0:T(8,128)} %fusion.295, bf16[4096,192]{0,1:T(8,128)(2,1)S(1)} %bitcast.337, bf16[768,192]{0,1:T(8,128)(2,1)S(1)} %copy-done.104), kind=kOutput, calls=%fused_computation.36 | convolution fusion | flops 1220542464 | bytes 33325056 | tf_op jit(solution)/shard_map/tc,dc->td/dot_general | solution.py:277
  584.3 11.1 %all-reduce.38 = (f32[768]{0:T(1024)}, f32[768]{0:T(1024)}, f32[768]{0:T(1024)}, f32[768]{0:T(1024)}) all-reduce(f32[768]{0:T(1024)S(1)} %copy-done.137, f32[768]{0:T(1024)S(1)} %copy-done.138, f32[768]{0:T(1024)S(1)} %copy-done.124, f32[768]{0:T(1024)S(1)} %copy-done.125), channel_id=1, replica_groups=mesh['batch'=8,'head'=4] {'head'}, use_global_device_ids=true, to_apply=%region_62.63 | all-reduce | flops 3072 | bytes 24576 | tf_op jit(solution)/shard_map/psum | solution.py:288
  595.4 8.3 fusion.117
  604.4 8.4 fusion.115
  628.9 8.3 fusion.113
  639.3 9.2 %fusion.111 = (f32[3]{0:T(128)}, f32[3]{0:T(128)}, f32[3]{0:T(128)}, f32[3]{0:T(128)}, f32[3]{0:T(128)}, /*index=5*/f32[3]{0:T(128)}, f32[3]{0:T(128)}, f32[3]{0:T(128)}) fusion(f32[4096]{0:T(1024)} %get-tuple-element.147, f32[4096,3,64]{0,2,1:T(8,128)S(1)} %copy-done.2, bf16[4096,3,64]{0,2,1:T(8,128)(2,1)} %bitcast.320, pred[4096]{0:T(1024)(128)(4,1)S(1)} %copy-done.91, ...), kind=kLoop, calls=%fused_computation.179 | loop fusion | flops 20447208 | bytes 4853856 | tf_op jit(solution)/shard_map/reduce_sum | solution.py:251
  656.3 209.2 %all-reduce.43 = (f32[3,33]{1,0:T(4,128)}, f32[768]{0:T(1024)}, f32[768]{0:T(1024)}, f32[768,768]{1,0:T(8,128)}, f32[768,768]{1,0:T(8,128)}, /*index=5*/f32[768]{0:T(1024)}, f32[768]{0:T(1024)}) all-reduce(f32[3,33]{1,0:T(4,128)S(1)} %stack.135, f32[768]{0:T(1024)} %get-tuple-element.110, ...), channel_id=1, replica_groups=mesh['batch'=8,'head'=4] {'batch'}, use_global_device_ids=true, to_apply=%region_60.61 | all-reduce | flops 1182819 | bytes 7103256 | tf_op jit(solution)/shard_map/psum | solution.py:284
  (535 shorter events, 199.4 us)
Async XLA Ops:
  7.2 172.6 %copy-start = (bf16[192,768]{1,0:T(8,128)(2,1)S(1)}, bf16[192,768]{1,0:T(8,128)(2,1)}, u32[]{:S(2)}) copy-start(bf16[192,768]{1,0:T(8,128)(2,1)} %param.23) | copy-start | bytes 884740
  7.2 51.5 %copy-start.107 = (bf16[768,192]{0,1:T(8,128)(2,1)S(1)}, bf16[768,192]{0,1:T(8,128)(2,1)}, u32[]{:S(2)}) copy-start(bf16[768,192]{0,1:T(8,128)(2,1)} %param.20) | copy-start | bytes 884740
  7.2 51.5 %all-gather.3.cloned.1.call-start = ((), (), s32[]{:S(2)}) async-start(), calls=%async_computation.4 | async-start | bytes 7864320 | tf_op jit(solution)/shard_map/all_gather | solution.py:72
  8.0 236.4 %reduce-scatter.5.cloned.1.call-start = ((), (), s32[]{:S(2)}) async-start(), calls=%async_computation.5 | async-start | bytes 7864320 | tf_op jit(solution)/shard_map/reduce_scatter | solution.py:157
  10.6 88.6 %copy-start.44 = (f32[64,64]{1,0:T(8,128)}, f32[64,64]{1,0:T(8,128)S(1)}, u32[]{:S(2)}) copy-start(f32[64,64]{1,0:T(8,128)S(1)} %get-tuple-element.173) | copy-start | bytes 49156
  11.4 56.1 %copy-start.90 = (pred[4096]{0:T(1024)(128)(4,1)}, pred[4096]{0:T(1024)(128)(4,1)S(1)}, u32[]{:S(2)}) copy-start(pred[4096]{0:T(1024)(128)(4,1)S(1)} %get-tuple-element.117) | copy-start | bytes 12292
  11.4 134.1 %copy-start.99 = (f32[4096]{0:T(1024)}, f32[4096]{0:T(1024)S(1)}, u32[]{:S(2)}) copy-start(f32[4096]{0:T(1024)S(1)} %get-tuple-element.116) | copy-start | bytes 49156
  12.1 55.3 %copy-start.96 = (s32[4096]{0:T(1024)}, s32[4096]{0:T(1024)S(1)}, u32[]{:S(2)}) copy-start(s32[4096]{0:T(1024)S(1)} %multiply_add_fusion.1) | copy-start | bytes 49156
  13.6 55.3 %copy-start.120 = (f32[256]{0:T(256)}, f32[256]{0:T(256)S(1)}, u32[]{:S(2)}) copy-start(f32[256]{0:T(256)S(1)} %convert_reduce_fusion.1) | copy-start | bytes 3076
  24.0 77.7 %copy-start.4 = (pred[256,4096]{1,0:T(8,128)(4,1)}, pred[256,4096]{1,0:T(8,128)(4,1)S(1)}, u32[]{:S(2)}) copy-start(pred[256,4096]{1,0:T(8,128)(4,1)S(1)} %compare_and_fusion) | copy-start | bytes 3145732
  68.9 61.3 %copy-start.75 = (bf16[256,3,64]{0,2,1:T(8,128)(2,1)}, bf16[256,3,64]{0,2,1:T(8,128)(2,1)S(1)}, u32[]{:S(2)}) copy-start(bf16[256,3,64]{0,2,1:T(8,128)(2,1)S(1)} %get-tuple-element.151) | copy-start | bytes 294916
  144.9 34.8 %copy-start.92 = (f32[3,4096]{1,0:T(4,128)}, f32[3,4096]{1,0:T(4,128)S(1)}, u32[]{:S(2)}) copy-start(f32[3,4096]{1,0:T(4,128)S(1)} %log_add_fusion) | copy-start | bytes 147460
  185.8 58.5 %copy-start.6 = (bf16[1024,768]{1,0:T(8,128)(2,1)S(1)}, bf16[1024,768]{1,0:T(8,128)(2,1)}, u32[]{:S(2)}) copy-start(bf16[1024,768]{1,0:T(8,128)(2,1)} %param.16) | copy-start | bytes 4718596
  185.8 61.3 %copy-start.122 = (f32[768]{0:T(1024)S(1)}, f32[768]{0:T(1024)}, u32[]{:S(2)}) copy-start(f32[768]{0:T(1024)} %param.25) | copy-start | bytes 9220
  185.8 61.3 %copy-start.141 = (f32[768]{0:T(1024)S(1)}, f32[768]{0:T(1024)}, u32[]{:S(2)}) copy-start(f32[768]{0:T(1024)} %param.26) | copy-start | bytes 9220
  185.8 190.7 %all-gather.5.cloned.1.call-start = ((), (), s32[]{:S(2)}) async-start(), calls=%async_computation.6 | async-start | bytes 7864320 | tf_op jit(solution)/shard_map/all_gather | solution.py:197
  244.3 40.4 %slice-start.13 = ((s8[4718592]{0:T(1024)(128)(4,1)}), s8[4194304]{0:T(1024)(128)(4,1)S(1)}, s32[]{:S(2)}) async-start(s8[4718592]{0:T(1024)(128)(4,1)} %bitcast.394), calls=%async_computation.24 | async-start | bytes 8388608
  246.4 119.6 %copy-start.112 = (f32[1024]{0:T(1024)}, f32[1024]{0:T(1024)S(1)}, u32[]{:S(2)}) copy-start(f32[1024]{0:T(1024)S(1)} %broadcast_multiply_fusion.5) | copy-start | bytes 12292
  247.2 118.8 %copy-start.114 = (f32[1024]{0:T(1024)}, f32[1024]{0:T(1024)S(1)}, u32[]{:S(2)}) copy-start(f32[1024]{0:T(1024)S(1)} %add_rsqrt_fusion.1) | copy-start | bytes 12292
  247.2 37.5 %slice-start.14 = ((s8[4718592]{0:T(1024)(128)(4,1)}), s8[524288]{0:T(1024)(128)(4,1)S(1)}, s32[]{:S(2)}) async-start(s8[4718592]{0:T(1024)(128)(4,1)} %bitcast.394), calls=%async_computation.25 | async-start | bytes 1048576
  329.8 326.4 %reduce-scatter.11.cloned.1.call-start = ((), (), s32[]{:S(2)}) async-start(), calls=%async_computation.9 | async-start | bytes 5898240 | tf_op jit(solution)/shard_map/reduce_scatter | solution.py:193
  342.0 314.2 %reduce-scatter.9.cloned.1.call-start = ((), (), s32[]{:S(2)}) async-start(), calls=%async_computation.8 | async-start | bytes 5898240 | tf_op jit(solution)/shard_map/reduce_scatter | solution.py:190
  376.3 489.2 %reduce-scatter.7.cloned.1.call-start = ((), (), s32[]{:S(2)}) async-start(), calls=%async_computation.7 | async-start | bytes 7864320 | tf_op jit(solution)/shard_map/reduce_scatter | solution.py:274
  383.1 128.3 %copy-start.3 = (bf16[4096,192]{0,1:T(8,128)(2,1)}, bf16[4096,192]{0,1:T(8,128)(2,1)S(1)}, u32[]{:S(2)}) copy-start(bf16[4096,192]{0,1:T(8,128)(2,1)S(1)} %get-tuple-element.172) | copy-start | bytes 4718596
  511.4 59.8 %copy-start.104 = (bf16[768,192]{0,1:T(8,128)(2,1)S(1)}, bf16[768,192]{0,1:T(8,128)(2,1)}, u32[]{:S(2)}) copy-start(bf16[768,192]{0,1:T(8,128)(2,1)} %param.22) | copy-start | bytes 884740
  583.7 286.3 %all-reduce.42.cloned.1.call-start = ((), (), s32[]{:S(2)}) async-start(), calls=%async_computation.10 | async-start | bytes 4718592 | tf_op jit(solution)/shard_map/psum | solution.py:284
  639.3 226.2 %copy-start.113 = (f32[1024]{0:T(1024)S(1)}, f32[1024]{0:T(1024)}, u32[]{:S(2)}) copy-start(f32[1024]{0:T(1024)} %copy-done.112) | copy-start | bytes 12292
  639.3 226.2 %copy-start.115 = (f32[1024]{0:T(1024)S(1)}, f32[1024]{0:T(1024)}, u32[]{:S(2)}) copy-start(f32[1024]{0:T(1024)} %copy-done.114) | copy-start | bytes 12292
  639.3 226.2 %copy-start.117 = (f32[1024]{0:T(1024)S(1)}, f32[1024]{0:T(1024)}, u32[]{:S(2)}) copy-start(f32[1024]{0:T(1024)} %copy-done.116) | copy-start | bytes 12292
  639.3 226.2 %copy-start.119 = (f32[1024]{0:T(1024)S(1)}, f32[1024]{0:T(1024)}, u32[]{:S(2)}) copy-start(f32[1024]{0:T(1024)} %copy-done.118) | copy-start | bytes 12292
  639.3 226.2 %copy-start.123 = (f32[768]{0:T(1024)S(1)}, f32[768]{0:T(1024)}, u32[]{:S(2)}) copy-start(f32[768]{0:T(1024)} %param.25) | copy-start | bytes 9220
  648.5 217.0 %copy-start.7 = (bf16[1024,768]{1,0:T(8,128)(2,1)S(1)}, bf16[1024,768]{1,0:T(8,128)(2,1)}, u32[]{:S(2)}) copy-start(bf16[1024,768]{1,0:T(8,128)(2,1)} %param.16) | copy-start | bytes 4718596
  (133 other events, 853.6 us)
Sparse Core Ops, SparseCore 0:
  9.6 49.0 all-gather.2
  185.9 58.3 reduce-scatter.4
  330.0 46.4 all-gather.4
  379.0 47.8 reduce-scatter.10
  429.3 47.8 reduce-scatter.8
  583.8 58.8 reduce-scatter.6
  647.1 170.6 all-reduce.41
